TPU v7x, 128 devices: a whole 4x4x4 slice. The times are simulated.
128 devices in a mesh: prow: 8 (over x, core), pcol: 16 (over z, y).
Axes of the slice: x: 4, y: 4, z: 4, core: 2. Of those that a mesh axis runs over, the one named last changes fastest.
Arguments:
- child_u: bfloat16 [2, 5, 8, 2, 16, 512, 128], P(None, None, 'prow', None, 'pcol'), may hold values from -5 to 5
- child_v: bfloat16 [2, 5, 8, 2, 16, 512, 128], P(None, None, 'prow', None, 'pcol'), may hold values from -5 to 5
- child_rank: int32 [2, 5, 8, 2, 16], P(None, None, 'prow', None, 'pcol'), may hold values from 0 to 128, as said below
- diag_shift: float32 [32, 512], replicated, may hold values from 0.5 to 4
Outputs:
- front_out: float32 [5, 8, 512, 2, 16, 512], P(None, 'prow', None, None, 'pcol')
Inputs may be any that keep to these rules, and one draw needn't show every extreme that they name: `child_rank`: 0 on and above the block diagonal (i <= j); below it 0 where the child has no tile, else from 16 to 128.
All inputs are finite; a program needn't handle non-finite values.
Results may differ from a plain program's by a relative error of at most 0.0003.
Values may be sent and summed in bfloat16 or wider, within the bound.
No kernel may reach another device: no remote copies, remote signals or barrier semaphores. Data moves between devices by JAX's collectives and lax.ppermute only.
A program may use at most 320 MiB of HBM per device.

v0:
```python
import jax
import jax.numpy as jnp
from jax import lax
from jax.sharding import PartitionSpec as P

PANELS = 2


def from_root(value, axis, root):
    return lax.dynamic_index_in_dim(lax.all_gather(value, axis), root, 0, keepdims=False)


def spread(value, axis, root):
    mine = lax.axis_index(axis) == root
    return lax.psum(jnp.where(mine, value, jnp.zeros_like(value)), axis)


def rows_for(lines, size):
    spare = -len(lines) % size
    return jnp.pad(lines, [(0, spare)] + [(0, 0)] * (lines.ndim - 1))


def sum_by_parts(value, axis):
    lines = value.reshape(-1, *value.shape[1:][-1:])
    padded = rows_for(lines, lax.axis_size(axis))
    own = lax.psum_scatter(padded, axis, scatter_dimension=0, tiled=True)
    whole = lax.all_gather(own, axis, axis=0, tiled=True)
    return whole[: len(lines)].reshape(value.shape)


def factor_panel(column, panel_index, block_rows, block_cols, own_column, prow_count, pcol_count):
    extent = column.shape[-1]
    pivot_tile = from_root(column[panel_index // prow_count], "prow", panel_index % prow_count)
    is_owner = own_column == panel_index % pcol_count
    pivot_tile = jnp.where(is_owner, pivot_tile, jnp.eye(extent, dtype=jnp.float32))
    factor = jnp.linalg.cholesky(pivot_tile)
    solved = lax.linalg.triangular_solve(
        factor, column.reshape(-1, extent), left_side=False, lower=True, transpose_a=True
    ).reshape(column.shape)
    below_mask = (block_rows > panel_index)[:, None, None]
    solved = jnp.where(below_mask, solved, 0.0)
    pivot_diag = jnp.diagonal(factor)
    at_pivot = (block_rows == panel_index)[:, None, None]
    panel_out = jnp.where(
        at_pivot, (factor * pivot_diag[None, :])[None], solved * pivot_diag[None, None, :]
    )
    rounded = solved.astype(jnp.bfloat16)
    received = spread(rounded, "pcol", panel_index % pcol_count)
    picked = jnp.take(received, block_cols // prow_count, axis=0)
    column_rows = from_root(picked, "prow", own_column % prow_count)
    return (received, column_rows, panel_out, is_owner)


def trailing(column, received, other_rows):
    return column - jnp.einsum(
        "rab,cb->rac", received, other_rows, preferred_element_type=jnp.float32
    )


def on_device(child_u, child_v, child_rank, diag_shift):
    prow_count = lax.axis_size("prow")
    pcol_count = lax.axis_size("pcol")
    own_row = lax.axis_index("prow")
    own_column = lax.axis_index("pcol")
    rank_grid = child_rank[:, :, 0, :, 0]
    rows_here = rank_grid.shape[1]
    cols_here = rank_grid.shape[2]
    extent = child_u.shape[-2]
    keep_mask = (
        jnp.arange(child_u.shape[-1], dtype=jnp.int32)[None, None, None, :]
        < rank_grid[:, :, :, None]
    ).astype(jnp.bfloat16)
    left_factor = child_u[:, :, 0, :, 0] * keep_mask[:, :, :, None, :]
    right_factor = child_v[:, :, 0, :, 0] * keep_mask[:, :, :, None, :]
    tile_grid = jnp.einsum(
        "crtak,crtbk->rtab", left_factor, right_factor, preferred_element_type=jnp.float32
    )
    row_terms = jnp.einsum(
        "crtak,crtbk->rab", left_factor, left_factor, preferred_element_type=jnp.float32
    )
    column_terms = jnp.einsum(
        "crtak,crtbk->tab", right_factor, right_factor, preferred_element_type=jnp.float32
    )
    row_sums = sum_by_parts(row_terms, "pcol")
    column_sums = lax.psum(column_terms, "prow")
    block_rows = jnp.arange(rows_here, dtype=jnp.int32) * prow_count + own_row
    block_cols = jnp.arange(cols_here, dtype=jnp.int32) * pcol_count + own_column
    slab_total = diag_shift.shape[0]
    select_cols = (block_cols[:, None] == jnp.arange(slab_total, dtype=jnp.int32)[None, :]).astype(
        jnp.float32
    )
    shift_cols = jnp.dot(select_cols, diag_shift, precision=lax.Precision.HIGHEST)
    identity = jnp.eye(extent, dtype=jnp.float32)
    diag_terms = (
        row_sums[:, None]
        + column_sums[None, :]
        + identity[None, None] * shift_cols[None, :, None, :]
    )
    on_diagonal = (block_rows[:, None] == block_cols[None, :])[:, :, None, None]
    tile_grid = tile_grid + jnp.where(on_diagonal, diag_terms, 0.0)
    columns = [tile_grid[:, column_index] for column_index in range(cols_here)]
    results = [jnp.zeros_like(columns[0]) for column_index in range(cols_here)]
    for panel_index in range(PANELS):
        local_col = panel_index // pcol_count
        received, column_rows, panel_out, is_owner = factor_panel(
            columns[local_col],
            panel_index,
            block_rows,
            block_cols,
            own_column,
            prow_count,
            pcol_count,
        )
        results[local_col] = jnp.where(is_owner, panel_out, results[local_col])
        columns = [
            trailing(columns[column_index], received, column_rows[column_index])
            for column_index in range(cols_here)
        ]
    outputs = []
    for column_index in range(cols_here):
        lower_mask = (block_rows >= block_cols[column_index])[:, None, None]
        finished = jnp.where(lower_mask, columns[column_index], 0.0)
        outputs.append(
            jnp.where(block_cols[column_index] < PANELS, results[column_index], finished)
        )
    stacked = jnp.stack(outputs, axis=1)
    return stacked.transpose(0, 2, 1, 3)[:, None, :, :, None, :]


def solution(mesh):
    placed = (
        P(None, None, "prow", None, "pcol", None, None),
        P(None, None, "prow", None, "pcol", None, None),
        P(None, None, "prow", None, "pcol"),
        P(),
    )
    return jax.shard_map(
        on_device,
        mesh=mesh,
        in_specs=placed,
        out_specs=P(None, "prow", None, None, "pcol", None),
        check_vma=False,
    )
```

profile of v0, /device:TPU:1, one launch (start us, length us, event | category | flops | bytes accessed | tf_op | source)
XLA Modules:
  0.0 967.2 jit_solution(4222597804145825684)
XLA Ops:
  8.3 6.5 fusion.31
  14.9 1.7 copy-done.9
  16.5 2.9 fusion.34
  19.5 76.8 %reduce-scatter.2.cloned.1.call-done = f32[160,512]{1,0:T(8,128)} async-done(((f32[2560,512]{1,0:T(8,128)}), f32[160,512]{1,0:T(8,128)}) %reduce-scatter.2.cloned.1.call-update) | async-done | bytes 327696 | tf_op jit(solution)/shard_map/reduce_scatter | solution.py:26
  97.4 2.7 copy.65
  100.4 3.1 broadcast_multiply_fusion
  103.6 5.7 fusion.32
  109.2 46.1 %all-gather.9.cloned.1.call-done = f32[2560,512]{1,0:T(8,128)} async-done(((f32[160,512]{1,0:T(8,128)}), f32[2560,512]{1,0:T(8,128)}) %all-gather.9.cloned.1.call-update) | async-done | bytes 5242896 | tf_op jit(solution)/shard_map/all_gather | solution.py:27
  155.3 7.9 bitcast_add_fusion
  163.2 4.1 copy-done.2
  168.6 5.9 slice.199
  174.5 43.5 %all-gather.13.cloned.1.call-done = f32[8,1,512,512]{3,2,1,0:T(8,128)} async-done(((f32[1,1,512,512]{3,2,1,0:T(8,128)}), f32[8,1,512,512]{3,2,1,0:T(8,128)}) %all-gather.13.cloned.1.call-update) | async-done | bytes 8388624 | tf_op jit(solution)/shard_map/all_gather | solution.py:10
  220.3 11.7 %cholesky.286 = f32[128,128]{1,0:T(8,128)S(1)} custom-call(f32[128,128]{1,0:T(8,128)S(1)} %cholesky.426), custom_call_target="Cholesky" | custom-call | tf_op jit(solution)/shard_map/jit(cholesky)/cholesky | solution.py:36
  232.1 9.8 %custom-call.31 = f32[1,128,128]{1,2,0:T(8,128)S(1)} custom-call(f32[1,128,128]{2,1,0:T(8,128)S(1)} %get-tuple-element.67), custom_call_target="InvertDiagBlocksLowerTriangular" | custom-call | tf_op jit(solution)/shard_map/jit(cholesky)/cholesky | solution.py:36
  244.5 11.7 %cholesky.305 = f32[128,128]{1,0:T(8,128)S(1)} custom-call(f32[128,128]{1,0:T(8,128)S(1)} %cholesky.430), custom_call_target="Cholesky" | custom-call | tf_op jit(solution)/shard_map/jit(cholesky)/cholesky | solution.py:36
  256.2 10.3 %custom-call.32 = f32[1,128,128]{1,2,0:T(8,128)S(1)} custom-call(f32[1,128,128]{2,1,0:T(8,128)S(1)} %get-tuple-element.64), custom_call_target="InvertDiagBlocksLowerTriangular" | custom-call | tf_op jit(solution)/shard_map/jit(cholesky)/cholesky | solution.py:36
  268.1 11.7 %cholesky.326 = f32[128,128]{1,0:T(8,128)S(1)} custom-call(f32[128,128]{1,0:T(8,128)S(1)} %cholesky.435), custom_call_target="Cholesky" | custom-call | tf_op jit(solution)/shard_map/jit(cholesky)/cholesky | solution.py:36
  279.8 9.8 %custom-call.33 = f32[1,128,128]{1,2,0:T(8,128)S(1)} custom-call(f32[1,128,128]{2,1,0:T(8,128)S(1)} %get-tuple-element.61), custom_call_target="InvertDiagBlocksLowerTriangular" | custom-call | tf_op jit(solution)/shard_map/jit(cholesky)/cholesky | solution.py:36
  291.1 11.9 %cholesky.343 = f32[128,128]{1,0:T(8,128)S(1)} custom-call(f32[128,128]{1,0:T(8,128)S(1)} %convolution_subtract_fusion.9), custom_call_target="Cholesky" | custom-call | tf_op jit(solution)/shard_map/jit(cholesky)/cholesky | solution.py:36
  308.9 8.4 while.4
  309.6 1.4 bitcast_dynamic-update-slice_fusion.4
  311.7 1.4 bitcast_dynamic-update-slice_fusion.4
  317.3 39.3 %custom-call.34 = f32[4,128,128]{1,2,0:T(8,128)S(1)} custom-call(f32[4,128,128]{2,1,0:T(8,128)S(1)} %get-tuple-element.22), custom_call_target="InvertDiagBlocksLowerTriangular" | custom-call | tf_op jit(solution)/shard_map/triangular_solve/custom-call.3 | solution.py:37
  356.6 2.7 fusion.37
  359.4 3.5 convolution_subtract_fusion.1
  364.3 4.4 convolution_subtract_fusion.3
  370.0 7.1 fusion.20
  378.4 2.6 pad_maximum_fusion
  380.9 5.9 copy.69
  386.8 4.7 fusion.23
  391.7 92.3 %all-reduce.7.cloned.1.call-done = bf16[5,512,512]{2,1,0:T(8,128)(2,1)} async-done(((bf16[5,512,512]{2,1,0:T(8,128)(2,1)}), bf16[5,512,512]{2,1,0:T(8,128)(2,1)}) %all-reduce.7.cloned.1.call-update) | async-done | bytes 2621456 | tf_op jit(solution)/shard_map/psum | solution.py:15
  484.0 3.5 gather_fusion.2
  487.5 2.3 broadcast_select_fusion.1
  489.9 49.6 %all-gather.15.cloned.1.call-done = bf16[16,512,512]{2,1,0:T(8,128)(2,1)} async-done(((bf16[2,512,512]{2,1,0:T(8,128)(2,1)}), bf16[16,512,512]{2,1,0:T(8,128)(2,1)}) %all-gather.15.cloned.1.call-update) | async-done | bytes 8388624 | tf_op jit(solution)/shard_map/all_gather | solution.py:10
  539.5 4.3 bitcast_subtract_fusion
  543.8 2.3 copy-done.3
  547.4 49.6 %all-gather.11.cloned.1.call-done = f32[8,512,512]{2,1,0:T(8,128)} async-done(((f32[1,512,512]{2,1,0:T(8,128)}), f32[8,512,512]{2,1,0:T(8,128)}) %all-gather.11.cloned.1.call-update) | async-done | bytes 8388624 | tf_op jit(solution)/shard_map/all_gather | solution.py:10
  599.3 11.7 %cholesky.358 = f32[128,128]{1,0:T(8,128)S(1)} custom-call(f32[128,128]{1,0:T(8,128)S(1)} %cholesky.439), custom_call_target="Cholesky" | custom-call | tf_op jit(solution)/shard_map/jit(cholesky)/cholesky | solution.py:36
  611.2 9.8 %custom-call.35 = f32[1,128,128]{1,2,0:T(8,128)S(1)} custom-call(f32[1,128,128]{2,1,0:T(8,128)S(1)} %get-tuple-element.57), custom_call_target="InvertDiagBlocksLowerTriangular" | custom-call | tf_op jit(solution)/shard_map/jit(cholesky)/cholesky | solution.py:36
  623.5 11.7 %cholesky.377 = f32[128,128]{1,0:T(8,128)S(1)} custom-call(f32[128,128]{1,0:T(8,128)S(1)} %cholesky.443), custom_call_target="Cholesky" | custom-call | tf_op jit(solution)/shard_map/jit(cholesky)/cholesky | solution.py:36
  635.3 10.2 %custom-call.36 = f32[1,128,128]{1,2,0:T(8,128)S(1)} custom-call(f32[1,128,128]{2,1,0:T(8,128)S(1)} %get-tuple-element.54), custom_call_target="InvertDiagBlocksLowerTriangular" | custom-call | tf_op jit(solution)/shard_map/jit(cholesky)/cholesky | solution.py:36
  647.1 11.7 %cholesky.398 = f32[128,128]{1,0:T(8,128)S(1)} custom-call(f32[128,128]{1,0:T(8,128)S(1)} %cholesky.448), custom_call_target="Cholesky" | custom-call | tf_op jit(solution)/shard_map/jit(cholesky)/cholesky | solution.py:36
  658.8 9.8 %custom-call.37 = f32[1,128,128]{1,2,0:T(8,128)S(1)} custom-call(f32[1,128,128]{2,1,0:T(8,128)S(1)} %get-tuple-element.51), custom_call_target="InvertDiagBlocksLowerTriangular" | custom-call | tf_op jit(solution)/shard_map/jit(cholesky)/cholesky | solution.py:36
  670.1 11.8 %cholesky.415 = f32[128,128]{1,0:T(8,128)S(1)} custom-call(f32[128,128]{1,0:T(8,128)S(1)} %convolution_subtract_fusion.8), custom_call_target="Cholesky" | custom-call | tf_op jit(solution)/shard_map/jit(cholesky)/cholesky | solution.py:36
  688.3 8.1 while.5
  696.4 39.3 %custom-call.38 = f32[4,128,128]{1,2,0:T(8,128)S(1)} custom-call(f32[4,128,128]{2,1,0:T(8,128)S(1)} %get-tuple-element.23), custom_call_target="InvertDiagBlocksLowerTriangular" | custom-call | tf_op jit(solution)/shard_map/triangular_solve/custom-call.3 | solution.py:37
  735.7 2.7 fusion.35
  738.5 3.5 convolution_subtract_fusion
  743.4 4.4 convolution_subtract_fusion.2
  749.1 6.9 fusion.17
  757.3 2.6 pad_maximum_fusion.1
  759.9 5.9 copy.72
  765.8 4.8 fusion.24
  770.7 92.4 %all-reduce.9.cloned.1.call-done = bf16[5,512,512]{2,1,0:T(8,128)(2,1)} async-done(((bf16[5,512,512]{2,1,0:T(8,128)(2,1)}), bf16[5,512,512]{2,1,0:T(8,128)(2,1)}) %all-reduce.9.cloned.1.call-update) | async-done | bytes 2621456 | tf_op jit(solution)/shard_map/psum | solution.py:15
  863.2 2.4 gather_fusion.3
  870.2 9.0 gather_fusion.1
  879.2 2.3 broadcast_multiply_fusion.1
  881.5 5.0 fusion.48
  886.5 8.5 gather_fusion
  895.2 21.1 %all-gather.17.cloned.1.call-done = bf16[16,512,512]{2,1,0:T(8,128)(2,1)} async-done(((bf16[2,512,512]{2,1,0:T(8,128)(2,1)}), bf16[16,512,512]{2,1,0:T(8,128)(2,1)}) %all-gather.17.cloned.1.call-update) | async-done | bytes 8388624 | tf_op jit(solution)/shard_map/all_gather | solution.py:10
  916.4 9.3 fusion.4
  925.7 7.2 select_bitcast_fusion
  932.9 6.3 maximum_bitcast_fusion
  939.3 20.1 %copy.73 = f32[5,1,512,2,1,512]{5,4,3,2,1,0:T(1,128)} copy(f32[5,1,512,2,1,512]{5,2,0,3,4,1:T(8,128)S(1)} %maximum_bitcast_fusion) | data formatting | bytes 20971520 | tf_op jit(solution)/shard_map/broadcast_in_dim | solution.py:127
  (160 shorter events, 53.3 us)
Async XLA Ops:
  7.4 92.9 %copy-start = (f32[32,512]{1,0:T(8,128)S(1)}, f32[32,512]{1,0:T(8,128)}, u32[]{:S(2)}) copy-start(f32[32,512]{1,0:T(8,128)} %param.12) | copy-start | bytes 196612
  7.4 88.9 %reduce-scatter.2.cloned.1.call-start = ((), (), s32[]{:S(2)}) async-start(), calls=%async_computation.1 | async-start | bytes 5570560 | tf_op jit(solution)/shard_map/reduce_scatter | solution.py:26
  14.8 1.7 copy-start.9
  14.8 94.4 %all-reduce.5.cloned.1.call-start = ((), (), s32[]{:S(2)}) async-start(), calls=%async_computation.3 | async-start | bytes 4194304 | tf_op jit(solution)/shard_map/psum | solution.py:85
  19.4 135.9 %all-gather.9.cloned.1.call-start = ((), (), s32[]{:S(2)}) async-start(), calls=%async_computation.2 | async-start | bytes 5570560 | tf_op jit(solution)/shard_map/all_gather | solution.py:27
  96.3 121.7 %all-gather.13.cloned.1.call-start = ((), (), s32[]{:S(2)}) async-start(), calls=%async_computation.7 | async-start | bytes 9437184 | tf_op jit(solution)/shard_map/all_gather | solution.py:10
  97.4 6.1 copy-start.7
  100.1 3.4 copy-start.10
  163.2 4.1 copy-start.2
  168.3 315.7 %all-reduce.7.cloned.1.call-start = ((), (), s32[]{:S(2)}) async-start(), calls=%async_computation.4 | async-start | bytes 5242880 | tf_op jit(solution)/shard_map/psum | solution.py:15
  218.0 1.2 slice-start.6
  220.2 11.7 %copy-start.11 = (f32[512,512]{1,0:T(8,128)}, f32[512,512]{1,0:T(8,128)S(1)}, u32[]{:S(2)}) copy-start(f32[512,512]{1,0:T(8,128)S(1)} %fusion.43) | copy-start | bytes 3145732
  307.6 56.6 %slice-start.4 = ((s8[5242880]{0:T(1024)(128)(4,1)}), s8[1048576]{0:T(1024)(128)(4,1)S(1)}, s32[]{:S(2)}) async-start(s8[5242880]{0:T(1024)(128)(4,1)} %bitcast.208), calls=%async_computation.14 | async-start | bytes 2097152
  356.6 7.6 slice-start.5
  391.6 147.9 %all-gather.15.cloned.1.call-start = ((), (), s32[]{:S(2)}) async-start(), calls=%async_computation.8 | async-start | bytes 9437184 | tf_op jit(solution)/shard_map/all_gather | solution.py:10
  484.0 55.5 %copy-start.4 = (bf16[5,512,512]{2,1,0:T(8,128)(2,1)S(1)}, bf16[5,512,512]{2,1,0:T(8,128)(2,1)}, u32[]{:S(2)}) copy-start(bf16[5,512,512]{2,1,0:T(8,128)(2,1)} %all-reduce.7.cloned.1.call-done) | copy-start | bytes 7864324
  489.9 107.2 %all-gather.11.cloned.1.call-start = ((), (), s32[]{:S(2)}) async-start(), calls=%async_computation.5 | async-start | bytes 9437184 | tf_op jit(solution)/shard_map/all_gather | solution.py:10
  543.8 2.4 copy-start.3
  547.2 315.9 %all-reduce.9.cloned.1.call-start = ((), (), s32[]{:S(2)}) async-start(), calls=%async_computation.6 | async-start | bytes 5242880 | tf_op jit(solution)/shard_map/psum | solution.py:15
  597.0 1.2 slice-start.7
  599.3 11.7 %copy-start.12 = (f32[512,512]{1,0:T(8,128)}, f32[512,512]{1,0:T(8,128)S(1)}, u32[]{:S(2)}) copy-start(f32[512,512]{1,0:T(8,128)S(1)} %fusion.42) | copy-start | bytes 3145732
  687.0 56.3 %slice-start = ((s8[5242880]{0:T(1024)(128)(4,1)}), s8[1048576]{0:T(1024)(128)(4,1)S(1)}, s32[]{:S(2)}) async-start(s8[5242880]{0:T(1024)(128)(4,1)} %bitcast.197), calls=%async_computation.10 | async-start | bytes 2097152
  735.7 7.6 slice-start.1
  770.7 145.7 %all-gather.17.cloned.1.call-start = ((), (), s32[]{:S(2)}) async-start(), calls=%async_computation.9 | async-start | bytes 9437184 | tf_op jit(solution)/shard_map/all_gather | solution.py:10
  866.7 14.8 %copy-start.5 = (bf16[5,512,512]{2,1,0:T(8,128)(2,1)S(1)}, bf16[5,512,512]{2,1,0:T(8,128)(2,1)}, u32[]{:S(2)}) copy-start(bf16[5,512,512]{2,1,0:T(8,128)(2,1)} %all-reduce.7.cloned.1.call-done) | copy-start | bytes 7864324
  886.5 8.5 copy-start.6
  895.0 30.7 %slice-start.2 = ((s8[5242880]{0:T(1024)(128)(4,1)}), s8[1048576]{0:T(1024)(128)(4,1)S(1)}, s32[]{:S(2)}) async-start(s8[5242880]{0:T(1024)(128)(4,1)} %bitcast.201), calls=%async_computation.12 | async-start | bytes 2097152
  916.3 9.4 slice-start.3
  916.3 9.4 copy-start.8
  916.3 9.4 copy-start.13
  939.3 20.1 %copy-start.1 = (f32[32,512]{1,0:T(8,128)S(1)}, f32[32,512]{1,0:T(8,128)}, u32[]{:S(2)}) copy-start(f32[32,512]{1,0:T(8,128)} %param.12) | copy-start | bytes 196612
Sparse Core Ops, SparseCore 0:
  14.9 81.2 reduce-scatter.1
  98.4 56.8 all-gather.8
  391.7 92.2 all-reduce.6
  770.8 92.2 all-reduce.8
Sparse Core Ops, SparseCore 1:
  19.5 66.9 all-reduce.4
  168.4 49.5 all-gather.12
  489.9 49.5 all-gather.14
  547.3 49.7 all-gather.10
  866.8 49.5 all-gather.16
where the time goes:
time: 973 us; the launch traced here: 967 us
  waiting for transfers between devices  472 us (49%)
  other arithmetic  281 us (29%)
  local copies, waits for them, and re-layouts  95.8 us (10%)
  matrix products  95.2 us (10%)
  between operations  22.5 us (2%)
    psum x2, waiting for transfers between devices, spread(): return lax.psum(jnp.where(mine, value, jnp.zeros_like(value)), axis)  185 us
    all_gather x4, waiting for transfers between devices, from_root(): lax.all_gather(value, axis)  164 us
    another operation x29, other arithmetic, factor_panel(): factor = jnp.linalg.cholesky(pivot_tile)  159 us
    another operation x7, other arithmetic, factor_panel(): lax.linalg.triangular_solve(factor, column.reshape(-1, extent), left_side...  86.3 us
    reduce_scatter x1, waiting for transfers between devices, sum_by_parts(): own = lax.psum_scatter(padded, axis, scatter_dimension=0, tiled=True)  76.8 us
    all_gather x1, waiting for transfers between devices, sum_by_parts(): whole = lax.all_gather(own, axis, axis=0, tiled=True)  46.1 us
    another operation x14, matrix products, factor_panel(): lax.linalg.triangular_solve(factor, column.reshape(-1, extent), left_side...  43.2 us
    another operation x29, local copies, waits for them, and re-layouts, factor_panel(): lax.linalg.triangular_solve(factor, column.reshape(-1, extent), left_side...  28.1 us
  transfers between devices with their start and end apart: 9, of which 8 were waited for; matrix products, arithmetic and copies ran while one was open for 5% of the time, Pallas kernels for 0%

commit v1 on v0

--- a/solution.py
+++ b/solution.py
@@ -12,7 +12,7 @@
 
 def spread(value, axis, root):
     mine = lax.axis_index(axis) == root
-    return lax.psum(jnp.where(mine, value, jnp.zeros_like(value)), axis)
+    return jnp.sum(lax.all_gather(jnp.where(mine, value, jnp.zeros_like(value)), axis), axis=0)
 
 
 def rows_for(lines, size):

time: 973 us -> 1320 us (1.36)
  waiting for transfers between devices: 472 us -> 767 us
  other arithmetic: 281 us -> 319 us
    all_gather x0 -> x2, waiting for transfers between devices: none -> 480 us  [spread(): lax.all_gather(jnp.where(mine, value, jnp.zeros_like(value)), axis)]
    psum x2 -> x0, waiting for transfers between devices: 185 us -> none  [spread(): return lax.psum(jnp.where(mine, value, jnp.zeros_like(value)), axis)]
    reduce_sum x0 -> x2, other arithmetic: none -> 30.1 us  [spread(): jnp.sum(lax.all_gather(jnp.where(mine, value, jnp.zeros_like(value)), axi...]
  transfers between devices with their start and end apart: 9 -> 9, of which waited for: 8 -> 8; matrix products, arithmetic and copies ran while one was open for 5% -> 4% of each run, Pallas kernels for 0% -> 0%
where the time goes in v1:
time: 1320 us
  waiting for transfers between devices  767 us (58%)
  other arithmetic  319 us (24%)
  local copies, waits for them, and re-layouts  106 us (8%)
  matrix products  100 us (8%)
  between operations  22.2 us (2%)
    all_gather x2, waiting for transfers between devices, spread(): lax.all_gather(jnp.where(mine, value, jnp.zeros_like(value)), axis)  480 us
    all_gather x4, waiting for transfers between devices, from_root(): lax.all_gather(value, axis)  164 us
    another operation x29, other arithmetic, factor_panel(): factor = jnp.linalg.cholesky(pivot_tile)  160 us
    another operation x7, other arithmetic, factor_panel(): lax.linalg.triangular_solve(factor, column.reshape(-1, extent), left_side...  87.7 us
    reduce_scatter x1, waiting for transfers between devices, sum_by_parts(): own = lax.psum_scatter(padded, axis, scatter_dimension=0, tiled=True)  76.7 us
    all_gather x1, waiting for transfers between devices, sum_by_parts(): whole = lax.all_gather(own, axis, axis=0, tiled=True)  46 us
    another operation x14, matrix products, factor_panel(): lax.linalg.triangular_solve(factor, column.reshape(-1, extent), left_side...  45.9 us
    another operation x29, local copies, waits for them, and re-layouts, factor_panel(): lax.linalg.triangular_solve(factor, column.reshape(-1, extent), left_side...  31.6 us
  transfers between devices with their start and end apart: 9, of which 8 were waited for; matrix products, arithmetic and copies ran while one was open for 4% of the time, Pallas kernels for 0%

profile of v1, /device:TPU:1, one launch (start us, length us, event | category | flops | bytes accessed | tf_op | source)
XLA Modules:
  0.0 1315.2 jit_solution(11130379635255964868)
XLA Ops:
  8.3 6.5 fusion.31
  16.5 2.9 fusion.34
  19.4 76.7 %reduce-scatter.2.cloned.1.call-done = f32[160,512]{1,0:T(8,128)} async-done(((f32[2560,512]{1,0:T(8,128)}), f32[160,512]{1,0:T(8,128)}) %reduce-scatter.2.cloned.1.call-update) | async-done | bytes 327696 | tf_op jit(solution)/shard_map/reduce_scatter | solution.py:26
  97.3 2.7 copy.55
  100.3 3.1 broadcast_multiply_fusion
  103.4 5.7 fusion.32
  109.1 46.0 %all-gather.11.cloned.1.call-done = f32[2560,512]{1,0:T(8,128)} async-done(((f32[160,512]{1,0:T(8,128)}), f32[2560,512]{1,0:T(8,128)}) %all-gather.11.cloned.1.call-update) | async-done | bytes 5242896 | tf_op jit(solution)/shard_map/all_gather | solution.py:27
  155.1 7.9 bitcast_add_fusion
  163.0 4.1 copy-done.2
  168.4 5.8 slice.199
  174.3 43.5 %all-gather.19.cloned.1.call-done = f32[8,1,512,512]{3,2,1,0:T(8,128)} async-done(((f32[1,1,512,512]{3,2,1,0:T(8,128)}), f32[8,1,512,512]{3,2,1,0:T(8,128)}) %all-gather.19.cloned.1.call-update) | async-done | bytes 8388624 | tf_op jit(solution)/shard_map/all_gather | solution.py:10
  220.1 11.7 cholesky.286
  231.9 9.8 custom-call.31
  244.3 11.7 cholesky.305
  256.0 10.3 custom-call.32
  267.9 11.7 cholesky.326
  279.6 9.8 custom-call.33
  290.9 11.9 cholesky.343
  308.7 8.3 while.4
  317.1 39.3 %custom-call.34 = f32[4,128,128]{1,2,0:T(8,128)S(1)} custom-call(f32[4,128,128]{2,1,0:T(8,128)S(1)} %get-tuple-element.22), custom_call_target="InvertDiagBlocksLowerTriangular" | custom-call | tf_op jit(solution)/shard_map/triangular_solve/custom-call.3 | solution.py:37
  356.4 2.7 fusion.37
  359.2 3.5 convolution_subtract_fusion.1
  364.1 4.4 convolution_subtract_fusion.3
  369.8 7.1 fusion.20
  378.2 2.5 pad_maximum_fusion
  380.7 5.9 copy.59
  386.6 4.8 fusion.23
  391.5 239.9 %all-gather.13.cloned.1.call-done = bf16[16,5,512,512]{3,2,1,0:T(8,128)(2,1)} async-done(((bf16[1,5,512,512]{3,2,1,0:T(8,128)(2,1)}), bf16[16,5,512,512]{3,2,1,0:T(8,128)(2,1)}) %all-gather.13.cloned.1.call-update) | async-done | bytes 41943056 | tf_op jit(solution)/shard_map/all_gather | solution.py:15
  631.5 14.2 %reduce_sum.24 = bf16[5,512,512]{2,1,0:T(8,128)(2,1)S(1)} reduce(bf16[16,5,512,512]{3,2,1,0:T(8,128)(2,1)} %all-gather.13.cloned.1.call-done, bf16[]{:T(256)} %constant.183.clone.1), dimensions={0}, to_apply=%region_10.13 | reduce | flops 19660800 | bytes 44564480 | tf_op jit(solution)/shard_map/reduce_sum | solution.py:15
  649.6 49.6 %all-gather.21.cloned.1.call-done = bf16[16,512,512]{2,1,0:T(8,128)(2,1)} async-done(((bf16[2,512,512]{2,1,0:T(8,128)(2,1)}), bf16[16,512,512]{2,1,0:T(8,128)(2,1)}) %all-gather.21.cloned.1.call-update) | async-done | bytes 8388624 | tf_op jit(solution)/shard_map/all_gather | solution.py:10
  699.2 4.3 bitcast_subtract_fusion
  707.1 49.6 %all-gather.15.cloned.1.call-done = f32[8,512,512]{2,1,0:T(8,128)} async-done(((f32[1,512,512]{2,1,0:T(8,128)}), f32[8,512,512]{2,1,0:T(8,128)}) %all-gather.15.cloned.1.call-update) | async-done | bytes 8388624 | tf_op jit(solution)/shard_map/all_gather | solution.py:10
  759.0 2.5 copy.72
  763.8 2.5 copy.61
  769.1 11.7 cholesky.358
  782.0 9.8 custom-call.35
  795.0 11.7 cholesky.377
  807.3 10.2 custom-call.36
  819.9 11.7 cholesky.398
  832.3 9.8 custom-call.37
  844.3 11.8 cholesky.415
  861.8 2.8 fusion.44
  864.7 11.6 while.5
  876.2 39.3 %custom-call.38 = f32[4,128,128]{1,2,0:T(8,128)S(1)} custom-call(f32[4,128,128]{2,1,0:T(8,128)S(1)} %get-tuple-element.23), custom_call_target="InvertDiagBlocksLowerTriangular" | custom-call | tf_op jit(solution)/shard_map/triangular_solve/custom-call.3 | solution.py:37
  915.6 2.6 fusion.35
  918.2 3.6 convolution_subtract_fusion
  923.1 5.8 convolution_subtract_fusion.2
  930.2 8.3 fusion.17
  939.8 2.5 pad_maximum_fusion.1
  942.3 5.9 copy.62
  948.2 4.8 fusion.24
  953.1 240.0 %all-gather.17.cloned.1.call-done = bf16[16,5,512,512]{3,2,1,0:T(8,128)(2,1)} async-done(((bf16[1,5,512,512]{3,2,1,0:T(8,128)(2,1)}), bf16[16,5,512,512]{3,2,1,0:T(8,128)(2,1)}) %all-gather.17.cloned.1.call-update) | async-done | bytes 41943056 | tf_op jit(solution)/shard_map/all_gather | solution.py:15
  1193.1 15.9 %reduce_sum.25 = bf16[5,512,512]{2,1,0:T(8,128)(2,1)} reduce(bf16[16,5,512,512]{3,2,1,0:T(8,128)(2,1)} %all-gather.17.cloned.1.call-done, bf16[]{:T(256)} %constant.183.clone.1), dimensions={0}, to_apply=%region_11.15 | reduce | flops 19660800 | bytes 44564480 | tf_op jit(solution)/shard_map/reduce_sum | solution.py:15
  1209.0 3.3 gather_fusion.3
  1212.3 2.4 broadcast_select_fusion
  1218.0 8.7 gather_fusion.1
  1226.7 2.4 broadcast_multiply_fusion.1
  1229.1 5.0 fusion.48
  1234.1 8.7 gather_fusion
  1243.0 21.4 %all-gather.23.cloned.1.call-done = bf16[16,512,512]{2,1,0:T(8,128)(2,1)} async-done(((bf16[2,512,512]{2,1,0:T(8,128)(2,1)}), bf16[16,512,512]{2,1,0:T(8,128)(2,1)}) %all-gather.23.cloned.1.call-update) | async-done | bytes 8388624 | tf_op jit(solution)/shard_map/all_gather | solution.py:10
  1264.4 9.3 fusion.4
  1273.8 7.2 select_bitcast_fusion
  1281.0 6.3 maximum_bitcast_fusion
  1287.3 20.1 %copy.65 = f32[5,1,512,2,1,512]{5,4,3,2,1,0:T(1,128)} copy(f32[5,1,512,2,1,512]{5,2,0,3,4,1:T(8,128)S(1)} %maximum_bitcast_fusion) | data formatting | bytes 20971520 | tf_op jit(solution)/shard_map/broadcast_in_dim | solution.py:127
  (152 shorter events, 75.2 us)
Async XLA Ops:
  7.4 92.7 %copy-start = (f32[32,512]{1,0:T(8,128)S(1)}, f32[32,512]{1,0:T(8,128)}, u32[]{:S(2)}) copy-start(f32[32,512]{1,0:T(8,128)} %param.12) | copy-start | bytes 196612
  7.4 88.7 %reduce-scatter.2.cloned.1.call-start = ((), (), s32[]{:S(2)}) async-start(), calls=%async_computation.1 | async-start | bytes 5570560 | tf_op jit(solution)/shard_map/reduce_scatter | solution.py:26
  14.7 1.7 copy-start.7
  14.7 94.3 %all-reduce.3.cloned.1.call-start = ((), (), s32[]{:S(2)}) async-start(), calls=%async_computation.3 | async-start | bytes 4194304 | tf_op jit(solution)/shard_map/psum | solution.py:85
  19.4 135.7 %all-gather.11.cloned.1.call-start = ((), (), s32[]{:S(2)}) async-start(), calls=%async_computation.2 | async-start | bytes 5570560 | tf_op jit(solution)/shard_map/all_gather | solution.py:27
  96.1 121.6 %all-gather.19.cloned.1.call-start = ((), (), s32[]{:S(2)}) async-start(), calls=%async_computation.7 | async-start | bytes 9437184 | tf_op jit(solution)/shard_map/all_gather | solution.py:10
  97.3 6.1 copy-start.6
  100.0 3.4 copy-start.8
  163.0 4.1 copy-start.2
  168.1 463.3 %all-gather.13.cloned.1.call-start = ((), (), s32[]{:S(2)}) async-start(), calls=%async_computation.4 | async-start | bytes 44564480 | tf_op jit(solution)/shard_map/all_gather | solution.py:15
  217.8 1.2 slice-start.4
  220.0 11.7 copy-start.9
  307.4 56.6 %slice-start.2 = ((s8[5242880]{0:T(1024)(128)(4,1)}), s8[1048576]{0:T(1024)(128)(4,1)S(1)}, s32[]{:S(2)}) async-start(s8[5242880]{0:T(1024)(128)(4,1)} %bitcast.208), calls=%async_computation.12 | async-start | bytes 2097152
  356.4 7.6 slice-start.3
  391.4 307.8 %all-gather.21.cloned.1.call-start = ((), (), s32[]{:S(2)}) async-start(), calls=%async_computation.8 | async-start | bytes 9437184 | tf_op jit(solution)/shard_map/all_gather | solution.py:10
  649.6 107.1 %all-gather.15.cloned.1.call-start = ((), (), s32[]{:S(2)}) async-start(), calls=%async_computation.5 | async-start | bytes 9437184 | tf_op jit(solution)/shard_map/all_gather | solution.py:10
  703.5 2.3 copy-start.3
  706.9 486.2 %all-gather.17.cloned.1.call-start = ((), (), s32[]{:S(2)}) async-start(), calls=%async_computation.6 | async-start | bytes 44564480 | tf_op jit(solution)/shard_map/all_gather | solution.py:15
  768.1 1.0 copy-start.10
  953.0 311.4 %all-gather.23.cloned.1.call-start = ((), (), s32[]{:S(2)}) async-start(), calls=%async_computation.9 | async-start | bytes 9437184 | tf_op jit(solution)/shard_map/all_gather | solution.py:10
  1234.1 8.7 copy-start.4
  1242.8 30.9 %slice-start = ((s8[5242880]{0:T(1024)(128)(4,1)}), s8[1048576]{0:T(1024)(128)(4,1)S(1)}, s32[]{:S(2)}) async-start(s8[5242880]{0:T(1024)(128)(4,1)} %bitcast.201), calls=%async_computation.10 | async-start | bytes 2097152
  1264.4 9.4 slice-start.1
  1264.4 9.4 copy-start.5
  1264.4 9.4 copy-start.11
  1287.3 20.1 %copy-start.1 = (f32[32,512]{1,0:T(8,128)S(1)}, f32[32,512]{1,0:T(8,128)}, u32[]{:S(2)}) copy-start(f32[32,512]{1,0:T(8,128)} %param.12) | copy-start | bytes 196612
Sparse Core Ops, SparseCore 0:
  14.9 81.1 reduce-scatter.1
  98.2 56.8 all-gather.10
  391.5 239.8 all-gather.12
  953.2 239.8 all-gather.16
Sparse Core Ops, SparseCore 1:
  19.4 66.9 all-reduce.2
  168.2 49.5 all-gather.18
  649.6 49.5 all-gather.20
  707.0 49.7 all-gather.14
  1214.8 49.5 all-gather.22
